TPU v7x, 128 devices: a whole 4x4x4 slice. The times are simulated.
128 devices in a mesh: gx: 4 (over y), gy: 8 (over z_lo, x), gz: 4 (over z_hi, core).
Axes of the slice: x: 4, y: 4, z: 4 (z_hi: 2, z_lo: 2; z = z_hi * 2 + z_lo), core: 2. Of those that a mesh axis runs over, the one named last changes fastest.
Arguments:
- solution: float32 [16, 64, 128, 512], P(None, 'gx', 'gy', 'gz'), may hold values from -6 to 6
- residual: float32 [16, 64, 128, 512], P(None, 'gx', 'gy', 'gz'), may hold values from -15 to 15, as said below
- direction: float32 [16, 64, 128, 512], P(None, 'gx', 'gy', 'gz'), may hold values from -13 to 13, as said below
- kappa_squared: float32 [64, 128, 512], P('gx', 'gy', 'gz'), may hold values from 0.02 to 0.2
- conductance: float32 [64, 128, 512], P('gx', 'gy', 'gz'), may hold values from 0.1 to 1
Outputs:
- new_solution: float32 [16, 64, 128, 512], P(None, 'gx', 'gy', 'gz')
- new_residual: float32 [16, 64, 128, 512], P(None, 'gx', 'gy', 'gz')
- new_direction: float32 [16, 64, 128, 512], P(None, 'gx', 'gy', 'gz')
Inputs may be any that keep to these rules, and one draw needn't show every extreme that they name: residual is drawn with a part that is independent for each sample and each cell. direction is correlated with residual, sample by sample.
All inputs are finite; a program needn't handle non-finite values.
Results may differ from a plain program's by a relative error of at most 0.0003.
Values sent between devices are 32-bit elements; how exact they have to be, the bound alone decides.
No kernel may reach another device: no remote copies, remote signals or barrier semaphores. Data moves between devices by JAX's collectives and lax.ppermute only.
A program may use at most 128 MiB of HBM per device.

v0:
```python
import jax
import jax.numpy as jnp
from jax import lax
from jax.sharding import PartitionSpec as P

ITERS = 2


def with_halo(block, sides, width):
    for axis, dim in sides:
        count = lax.axis_size(axis)
        forward = [(i, i + 1) for i in range(count - 1)]
        backward = [(target, source) for source, target in forward]
        low = lax.ppermute(
            lax.slice_in_dim(block, block.shape[dim] - width, None, axis=dim), axis, forward
        )
        high = lax.ppermute(lax.slice_in_dim(block, 0, width, axis=dim), axis, backward)
        block = jnp.concatenate([low, block, high], axis=dim)
    return block


def six_sides(array):
    return [
        array[..., 2:, 1:-1, 1:-1],
        array[..., :-2, 1:-1, 1:-1],
        array[..., 1:-1, 2:, 1:-1],
        array[..., 1:-1, :-2, 1:-1],
        array[..., 1:-1, 1:-1, 2:],
        array[..., 1:-1, 1:-1, :-2],
    ]


def laplace(padded, kappa, conduct):
    centre = padded[..., 1:-1, 1:-1, 1:-1]
    conduct_mid = conduct[1:-1, 1:-1, 1:-1]
    total = kappa * centre
    for beside, face_dif in zip(six_sides(padded), six_sides(conduct)):
        total = total + 0.5 * (conduct_mid + face_dif) * (centre - beside)
    return total


def local_gram(first, second, count):
    return (
        jnp.dot(
            first.reshape(first.shape[0], -1),
            second.reshape(second.shape[0], -1).T,
            precision=lax.Precision.HIGHEST,
        )
        / count
    )


def symmetric(matrix):
    return 0.5 * (matrix + matrix.T)


def spd_solve(matrix, right):
    factor = jnp.linalg.cholesky(matrix)
    inner = lax.linalg.triangular_solve(factor, right, left_side=True, lower=True)
    return lax.linalg.triangular_solve(factor, inner, left_side=True, lower=True, transpose_a=True)


def combine(matrix, fields):
    flat = fields.reshape(fields.shape[0], -1)
    return jnp.dot(matrix, flat, precision=lax.Precision.HIGHEST).reshape(fields.shape)


def single_pass(field, kappa, conduct):
    padded = with_halo(field, (("gx", 1), ("gy", 2), ("gz", 3)), 1)
    return laplace(padded, kappa, conduct)


def body(solution, residual, direction, kappa_squared, conductance):
    samples, cells_x, cells_y, cells_z = direction.shape
    devices_all = lax.axis_size("gx") * lax.axis_size("gy") * lax.axis_size("gz")
    count = jnp.float32(cells_x * cells_y * cells_z * devices_all)
    coefs = with_halo(jnp.stack([kappa_squared, conductance]), (("gx", 1), ("gy", 2), ("gz", 3)), 2)
    kappa_mid = coefs[0, 2:-2, 2:-2, 2:-2]
    conduct_one = coefs[1, 1:-1, 1:-1, 1:-1]
    identity = jnp.eye(samples, dtype=jnp.float32)
    for iteration in range(ITERS):
        middle = single_pass(direction, kappa_mid, conduct_one)
        image = single_pass(middle, kappa_mid, conduct_one)
        dir_img, dir_res = lax.psum(
            (local_gram(direction, image, count), local_gram(direction, residual, count)),
            ("gx", "gy", "gz"),
        )
        curvature = symmetric(dir_img)
        step_mat = spd_solve(curvature, dir_res)
        solution = solution + combine(step_mat.T, direction)
        residual = residual - combine(step_mat.T, image)
        img_new = lax.psum(local_gram(image, residual, count), ("gx", "gy", "gz"))
        correction = -spd_solve(curvature, img_new)
        fresh = residual + combine(correction.T, direction)
        norms_mat = lax.psum(local_gram(fresh, fresh, count), ("gx", "gy", "gz"))
        factor = jnp.linalg.cholesky(symmetric(norms_mat))
        inverse = lax.linalg.triangular_solve(factor, identity, left_side=True, lower=True)
        direction = combine(inverse, fresh)
    return (solution, residual, direction)


def solution(mesh):
    in_specs = (
        P(None, "gx", "gy", "gz"),
        P(None, "gx", "gy", "gz"),
        P(None, "gx", "gy", "gz"),
        P("gx", "gy", "gz"),
        P("gx", "gy", "gz"),
    )
    out_specs = (P(None, "gx", "gy", "gz"), P(None, "gx", "gy", "gz"), P(None, "gx", "gy", "gz"))
    return jax.shard_map(body, mesh=mesh, in_specs=in_specs, out_specs=out_specs, check_vma=False)
```

profile of v0, /device:TPU:1, one launch (start us, length us, event | category | flops | bytes accessed | tf_op | source)
XLA Modules:
  0.0 767.0 jit_solution(1931507717396356238)
XLA Ops:
  27.1 4.6 collective-permute-start.9
  32.0 9.8 %collective-permute-start.4 = (f32[2,20,20,2]{3,2,1,0:T(8,128)S(1)}, f32[2,20,20,2]{3,2,1,0:T(8,128)S(1)}, u32[]{:S(2)}, u32[]{:S(2)}) collective-permute-start(f32[2,20,20,2]{3,2,1,0:T(8,128)S(1)} %get-tuple-element.58), channel_id=1, source_target_pairs={{0,1},{1,2},{2,3},{4,5},{5,6},{6,7},{8,9},{9,10},{10,11},{12,13},{... | collective-permute-start | bytes 19208 | tf_op jit(solution)/shard_map/ppermute | solution.py:14
  43.7 4.8 collective-permute-done.4
  48.5 4.9 collective-permute-done.5
  69.7 5.1 collective-permute-start.11
  79.1 4.1 copy.549
  83.2 8.6 %fusion.64 = f32[16,16,16,128]{3,2,1,0:T(8,128)S(1)} fusion(f32[16,16,16,128]{3,2,1,0:T(8,128)S(1)} %copy-done, f32[16,18,18,1]{3,2,1,0:T(8,128)} %copy.549, f32[16,18,1,128]{3,2,1,0:T(1,128)S(1)} %copy-done.20, f32[16,18,16,128]{3,2,1,0:T(8,128)} %copy-done.13, f32[16,18,1,128]{3,2,1,0:T(1,128)S(1)} %copy-done.22, f32[16,18,18,1]{3,2,1,0:T(8,128)} %copy.547, ...), kind=kLoop, calls=%fused_computation.119 | loop fusion | flops 15204352 | bytes 8069632 | tf_op jit(solution)/shard_map/add | solution.py:38
  100.7 4.3 collective-permute-start.15
  123.1 5.1 collective-permute-start.17
  128.3 6.3 fusion.139
  137.5 4.2 copy.557
  141.7 4.1 copy.559
  145.7 12.2 %fusion.46 = f32[16,16,16,128]{3,2,1,0:T(8,128)S(1)} fusion(f32[16,16,16,128]{3,2,1,0:T(8,128)} %copy-done.4, f32[16,18,18,1]{3,2,1,0:T(8,128)} %copy.559, f32[16,18,1,128]{3,2,1,0:T(1,128)S(1)} %copy.551, f32[16,18,1,128]{3,2,1,0:T(1,128)S(1)} %copy.553, f32[16,1,16,128]{3,2,1,0:T(8,128)S(1)} %collective-permute-done.12, f32[16,1,16,128]{3,2,1,0:T(8,128)} %copy-done.24, ...), kind=kLoop, calls=%fused_computation.83 | loop fusion | flops 19398656 | bytes 5710336 | tf_op jit(solution)/shard_map/add | solution.py:38
  157.9 4.8 fusion.149
  165.7 72.3 %all-reduce.1 = (f32[16,16]{1,0:T(8,128)S(1)}, f32[16,16]{0,1:T(8,128)S(1)}) all-reduce(f32[16,16]{1,0:T(8,128)S(1)} %fusion.139, f32[16,16]{0,1:T(8,128)S(1)} %fusion.149), channel_id=1, replica_groups=mesh['gx'=4,'gy'=8,'gz'=4] {'gx','gy','gz'}, use_global_device_ids=true, to_apply=%region_3.0 | all-reduce | flops 512 | bytes 4096 | tf_op jit(solution)/shard_map/psum | solution.py:84
  242.5 6.2 copy_subtract_fusion
  252.3 63.0 %psum.58 = f32[16,16]{1,0:T(8,128)S(1)} all-reduce(f32[16,16]{1,0:T(8,128)S(1)} %fusion.154), channel_id=1, replica_groups=mesh['gx'=4,'gy'=8,'gz'=4] {'gx','gy','gz'}, use_global_device_ids=true, to_apply=%region_4.8 | all-reduce | flops 256 | bytes 2048 | tf_op jit(solution)/shard_map/psum | solution.py:92
  315.7 4.4 fusion.103
  325.1 64.1 %psum.59 = f32[16,16]{1,0:T(8,128)S(1)} all-reduce(f32[16,16]{1,0:T(8,128)S(1)} %fusion.134), channel_id=1, replica_groups=mesh['gx'=4,'gy'=8,'gz'=4] {'gx','gy','gz'}, use_global_device_ids=true, to_apply=%region_5.9 | all-reduce | flops 256 | bytes 2048 | tf_op jit(solution)/shard_map/psum | solution.py:95
  393.5 4.4 fusion.5
  422.5 5.1 collective-permute-start.22
  438.7 4.1 copy.589
  442.8 9.5 %fusion.28 = f32[16,16,16,128]{3,2,1,0:T(8,128)S(1)} fusion(f32[16,16,16,128]{3,2,1,0:T(8,128)} %bitcast.244, f32[16,18,18,1]{3,2,1,0:T(8,128)} %copy.589, f32[16,18,1,128]{3,2,1,0:T(1,128)S(1)} %copy.581, f32[16,18,16,128]{3,2,1,0:T(8,128)} %copy-done.14, f32[16,18,1,128]{3,2,1,0:T(1,128)S(1)} %copy.583, f32[16,18,18,1]{3,2,1,0:T(8,128)} %copy.587, ...), kind=kLoop, calls=%fused_computation.55 | loop fusion | flops 15204352 | bytes 8069632 | tf_op jit(solution)/shard_map/add | solution.py:38
  462.0 4.7 collective-permute-start.27
  489.4 5.0 fusion.130
  498.5 4.1 copy.599
  502.5 11.4 %fusion.10 = f32[16,16,16,128]{3,2,1,0:T(8,128)S(1)} fusion(f32[16,16,16,128]{3,2,1,0:T(8,128)} %copy-done.3, f32[16,18,18,1]{3,2,1,0:T(8,128)} %copy.599, f32[16,18,1,128]{3,2,1,0:T(1,128)S(1)} %copy.591, f32[16,18,1,128]{3,2,1,0:T(1,128)S(1)} %copy.593, f32[16,1,16,128]{3,2,1,0:T(8,128)S(1)} %collective-permute-done.24, f32[16,1,16,128]{3,2,1,0:T(8,128)} %copy-done.23, ...), kind=kLoop, calls=%fused_computation.19 | loop fusion | flops 19398656 | bytes 5710336 | tf_op jit(solution)/shard_map/add | solution.py:38
  520.5 70.3 %all-reduce = (f32[16,16]{1,0:T(8,128)S(1)}, f32[16,16]{1,0:T(8,128)S(1)}) all-reduce(f32[16,16]{1,0:T(8,128)S(1)} %fusion.130, f32[16,16]{1,0:T(8,128)S(1)} %fusion.127), channel_id=1, replica_groups=mesh['gx'=4,'gy'=8,'gz'=4] {'gx','gy','gz'}, use_global_device_ids=true, to_apply=%region_7.11 | all-reduce | flops 512 | bytes 4096 | tf_op jit(solution)/shard_map/psum | solution.py:84
  595.5 5.2 fusion.108
  605.6 64.2 %psum.62 = f32[16,16]{1,0:T(8,128)S(1)} all-reduce(f32[16,16]{1,0:T(8,128)S(1)} %fusion.136), channel_id=1, replica_groups=mesh['gx'=4,'gy'=8,'gz'=4] {'gx','gy','gz'}, use_global_device_ids=true, to_apply=%region_8.12 | all-reduce | flops 256 | bytes 2048 | tf_op jit(solution)/shard_map/psum | solution.py:92
  685.2 63.0 %psum.63 = f32[16,16]{1,0:T(8,128)S(1)} all-reduce(f32[16,16]{1,0:T(8,128)S(1)} %fusion.133), channel_id=1, replica_groups=mesh['gx'=4,'gy'=8,'gz'=4] {'gx','gy','gz'}, use_global_device_ids=true, to_apply=%region_9.13 | all-reduce | flops 256 | bytes 2048 | tf_op jit(solution)/shard_map/psum | solution.py:95
  759.6 5.0 copy_add_fusion.1
  (239 shorter events, 216.2 us)
Async XLA Ops:
  1.6 5.3 collective-permute-start
  5.6 4.7 collective-permute-start.1
  11.2 9.9 %collective-permute-start.2 = (f32[2,20,2,128]{3,2,1,0:T(2,128)S(1)}, f32[2,20,2,128]{3,2,1,0:T(2,128)S(1)}, u32[]{:S(2)}, u32[]{:S(2)}) collective-permute-start(f32[2,20,2,128]{3,2,1,0:T(2,128)S(1)} %get-tuple-element.66), channel_id=1, source_target_pairs={{0,4},{4,8},{8,12},{12,16},{16,20},{20,24},{24,28},{1,5},{5,9},{9,... | collective-permute-start | bytes 122888 | tf_op jit(solution)/shard_map/ppermute | solution.py:14
  14.3 6.8 collective-permute-start.3
  16.6 5.6 collective-permute-start.7
  19.9 5.7 collective-permute-start.6
  22.9 30.5 %copy-start.17 = (f32[16,16,128]{2,1,0:T(8,128)S(1)}, f32[16,16,128]{2,1,0:T(8,128)}, u32[]{:S(2)}) copy-start(f32[16,16,128]{2,1,0:T(8,128)} %param.14) | copy-start | bytes 393220
  25.8 28.0 %collective-permute-start.8 = (f32[16,18,1,128]{3,0,2,1:T(8,128)S(1)}, f32[16,18,1,128]{3,0,2,1:T(8,128)S(1)}, u32[]{:S(2)}, u32[]{:S(2)}) collective-permute-start(f32[16,18,1,128]{3,0,2,1:T(8,128)S(1)} %copy.630), channel_id=1, source_target_pairs={{4,0},{8,4},{12,8},{16,12},{20,16},{24,20},{28,24},{5,1},{9,5},{13... | collective-permute-start | bytes 442376 | tf_op jit(solution)/shard_map/ppermute | solution.py:17
  27.1 26.8 %collective-permute-start.9 = (f32[16,18,1,128]{3,0,2,1:T(8,128)S(1)}, f32[16,18,1,128]{3,0,2,1:T(8,128)S(1)}, u32[]{:S(2)}, u32[]{:S(2)}) collective-permute-start(f32[16,18,1,128]{3,0,2,1:T(8,128)S(1)} %copy.631), channel_id=1, source_target_pairs={{0,4},{4,8},{8,12},{12,16},{16,20},{20,24},{24,28},{1,5},{5,9},{9,... | collective-permute-start | bytes 442376 | tf_op jit(solution)/shard_map/ppermute | solution.py:14
  32.0 16.5 %collective-permute-start.4 = (f32[2,20,20,2]{3,2,1,0:T(8,128)S(1)}, f32[2,20,20,2]{3,2,1,0:T(8,128)S(1)}, u32[]{:S(2)}, u32[]{:S(2)}) collective-permute-start(f32[2,20,20,2]{3,2,1,0:T(8,128)S(1)} %get-tuple-element.58), channel_id=1, source_target_pairs={{0,1},{1,2},{2,3},{4,5},{5,6},{6,7},{8,9},{9,10},{10,11},{12,13},{... | collective-permute-start | bytes 19208 | tf_op jit(solution)/shard_map/ppermute | solution.py:14
  41.7 11.7 %collective-permute-start.5 = (f32[2,20,20,2]{3,2,1,0:T(8,128)S(1)}, f32[2,20,20,2]{3,2,1,0:T(8,128)S(1)}, u32[]{:S(2)}, u32[]{:S(2)}) collective-permute-start(f32[2,20,20,2]{3,2,1,0:T(8,128)S(1)} %get-tuple-element.59), channel_id=1, source_target_pairs={{1,0},{2,1},{3,2},{5,4},{6,5},{7,6},{9,8},{10,9},{11,10},{13,12},{... | collective-permute-start | bytes 19208 | tf_op jit(solution)/shard_map/ppermute | solution.py:17
  63.8 11.3 %collective-permute-start.10 = (f32[16,18,18,1]{2,0,3,1:T(8,128)}, f32[16,18,18,1]{2,0,3,1:T(8,128)}, u32[]{:S(2)}, u32[]{:S(2)}) collective-permute-start(f32[16,18,18,1]{2,0,3,1:T(8,128)} %copy.546), channel_id=1, source_target_pairs={{1,0},{2,1},{3,2},{5,4},{6,5},{7,6},{9,8},{10,9},{11,10},{13,12},{... | collective-permute-start | bytes 62216 | tf_op jit(solution)/shard_map/ppermute | solution.py:17
  69.7 9.4 %collective-permute-start.11 = (f32[16,18,18,1]{2,0,3,1:T(8,128)}, f32[16,18,18,1]{2,0,3,1:T(8,128)}, u32[]{:S(2)}, u32[]{:S(2)}) collective-permute-start(f32[16,18,18,1]{2,0,3,1:T(8,128)} %copy.548), channel_id=1, source_target_pairs={{0,1},{1,2},{2,3},{4,5},{5,6},{6,7},{8,9},{9,10},{10,11},{12,13},{... | collective-permute-start | bytes 62216 | tf_op jit(solution)/shard_map/ppermute | solution.py:14
  91.8 5.7 collective-permute-start.12
  93.1 6.0 collective-permute-start.13
  99.3 7.0 collective-permute-start.14
  100.7 7.4 collective-permute-start.15
  116.8 20.8 %collective-permute-start.16 = (f32[16,18,18,1]{2,0,3,1:T(8,128)}, f32[16,18,18,1]{2,0,3,1:T(8,128)}, u32[]{:S(2)}, u32[]{:S(2)}) collective-permute-start(f32[16,18,18,1]{2,0,3,1:T(8,128)} %copy.556), channel_id=1, source_target_pairs={{1,0},{2,1},{3,2},{5,4},{6,5},{7,6},{9,8},{10,9},{11,10},{13,12},{... | collective-permute-start | bytes 62216 | tf_op jit(solution)/shard_map/ppermute | solution.py:17
  123.1 18.5 %collective-permute-start.17 = (f32[16,18,18,1]{2,0,3,1:T(8,128)}, f32[16,18,18,1]{2,0,3,1:T(8,128)}, u32[]{:S(2)}, u32[]{:S(2)}) collective-permute-start(f32[16,18,18,1]{2,0,3,1:T(8,128)} %copy.558), channel_id=1, source_target_pairs={{0,1},{1,2},{2,3},{4,5},{5,6},{6,7},{8,9},{9,10},{10,11},{12,13},{... | collective-permute-start | bytes 62216 | tf_op jit(solution)/shard_map/ppermute | solution.py:14
  248.7 67.0 %copy-start.1 = (f32[16,16,16,128]{3,0,2,1:T(8,128)}, f32[16,16,16,128]{3,0,2,1:T(8,128)S(1)}, u32[]{:S(2)}) copy-start(f32[16,16,16,128]{3,0,2,1:T(8,128)S(1)} %copy_subtract_fusion) | copy-start | bytes 6291460
  398.3 3.2 collective-permute-start.19
  399.6 5.9 collective-permute-start.18
  406.4 5.9 collective-permute-start.20
  407.9 5.9 collective-permute-start.21
  422.5 12.2 %collective-permute-start.22 = (f32[16,18,18,1]{2,0,3,1:T(8,128)}, f32[16,18,18,1]{2,0,3,1:T(8,128)}, u32[]{:S(2)}, u32[]{:S(2)}) collective-permute-start(f32[16,18,18,1]{2,0,3,1:T(8,128)} %copy.586), channel_id=1, source_target_pairs={{1,0},{2,1},{3,2},{5,4},{6,5},{7,6},{9,8},{10,9},{11,10},{13,12},{... | collective-permute-start | bytes 62216 | tf_op jit(solution)/shard_map/ppermute | solution.py:17
  431.6 7.1 collective-permute-start.23
  452.3 7.2 collective-permute-start.24
  453.9 6.6 collective-permute-start.25
  460.7 8.0 %collective-permute-start.26 = (f32[16,18,1,128]{3,0,2,1:T(8,128)S(1)}, f32[16,18,1,128]{3,0,2,1:T(8,128)S(1)}, u32[]{:S(2)}, u32[]{:S(2)}) collective-permute-start(f32[16,18,1,128]{3,0,2,1:T(8,128)S(1)} %copy.590), channel_id=1, source_target_pairs={{4,0},{8,4},{12,8},{16,12},{20,16},{24,20},{28,24},{5,1},{9,5},{13... | collective-permute-start | bytes 442376 | tf_op jit(solution)/shard_map/ppermute | solution.py:17
  462.0 6.9 collective-permute-start.27
  477.6 16.9 %collective-permute-start.28 = (f32[16,18,18,1]{2,0,3,1:T(8,128)}, f32[16,18,18,1]{2,0,3,1:T(8,128)}, u32[]{:S(2)}, u32[]{:S(2)}) collective-permute-start(f32[16,18,18,1]{2,0,3,1:T(8,128)} %copy.596), channel_id=1, source_target_pairs={{1,0},{2,1},{3,2},{5,4},{6,5},{7,6},{9,8},{10,9},{11,10},{13,12},{... | collective-permute-start | bytes 62216 | tf_op jit(solution)/shard_map/ppermute | solution.py:17
  485.4 13.1 %collective-permute-start.29 = (f32[16,18,18,1]{2,0,3,1:T(8,128)}, f32[16,18,18,1]{2,0,3,1:T(8,128)}, u32[]{:S(2)}, u32[]{:S(2)}) collective-permute-start(f32[16,18,18,1]{2,0,3,1:T(8,128)} %copy.598), channel_id=1, source_target_pairs={{0,1},{1,2},{2,3},{4,5},{5,6},{6,7},{8,9},{9,10},{10,11},{12,13},{... | collective-permute-start | bytes 62216 | tf_op jit(solution)/shard_map/ppermute | solution.py:14
  (27 other events, 228.2 us)
where the time goes:
time: 777 us; the launch traced here: 767 us
  blocking collectives  397 us (51%)
  local copies, waits for them, and re-layouts  113 us (15%)
  starting transfers between devices  92.7 us (12%)
  matrix products  67.4 us (9%)
  other arithmetic  65.2 us (8%)
  waiting for transfers between devices  29.5 us (4%)
    psum x2, blocking collectives, body(): lax.psum((local_gram(direction, image, count), local_gram(direction, resi...  143 us
    psum x2, blocking collectives, body(): img_new = lax.psum(local_gram(image, residual, count), ('gx', 'gy', 'gz'))  127 us
    psum x2, blocking collectives, body(): norms_mat = lax.psum(local_gram(fresh, fresh, count), ('gx', 'gy', 'gz'))  127 us
    ppermute x15, starting transfers between devices, with_halo(): lax.ppermute(lax.slice_in_dim(block, block.shape[dim] - width, None, axis...  64.2 us
    add x4, other arithmetic, laplace(): total = total + 0.5 * (conduct_mid + face_dif) * (centre - beside)  41.7 us
    dot_general x8, matrix products, combine(): jnp.dot(matrix, flat, precision=lax.Precision.HIGHEST).reshape(fields.shape)  33.2 us
    slice x12, local copies, waits for them, and re-layouts, with_halo(): lax.slice_in_dim(block, 0, width, axis=dim)  32.8 us
    dot_general x8, matrix products, local_gram(): jnp.dot(first.reshape(first.shape[0], -1), second.reshape(second.shape[0]...  32.4 us
  transfers between devices with their start and end apart: 30, of which 14 were waited for; matrix products, arithmetic and copies ran while one was open for 7% of the time, Pallas kernels for 0%

commit v1 on v0

--- a/solution.py
+++ b/solution.py
@@ -1,9 +1,18 @@
+import functools
 import jax
 import jax.numpy as jnp
 from jax import lax
 from jax.sharding import PartitionSpec as P
 
 ITERS = 2
+
+
+def _rest_windows(view, axis_id):
+    inter = jnp.sum(lax.all_gather(view, axis_id), axis=0)
+    return inter
+
+
+lead_blocks = functools.partial(_rest_windows, axis_id=("gx", "gy", "gz"))
 
 
 def with_halo(block, sides, width):
@@ -92,7 +101,7 @@
         img_new = lax.psum(local_gram(image, residual, count), ("gx", "gy", "gz"))
         correction = -spd_solve(curvature, img_new)
         fresh = residual + combine(correction.T, direction)
-        norms_mat = lax.psum(local_gram(fresh, fresh, count), ("gx", "gy", "gz"))
+        norms_mat = lead_blocks(local_gram(fresh, fresh, count))
         factor = jnp.linalg.cholesky(symmetric(norms_mat))
         inverse = lax.linalg.triangular_solve(factor, identity, left_side=True, lower=True)
         direction = combine(inverse, fresh)

time: 777 us -> 997 us (1.28)
  blocking collectives: 397 us -> 618 us
    all_gather x0 -> x2, blocking collectives: none -> 353 us  [_rest_windows(): inter = jnp.sum(lax.all_gather(view, axis_id), axis=0)]
    psum x2 -> x0, blocking collectives: 127 us -> none  [body(): norms_mat = lax.psum(local_gram(fresh, fresh, count), ('gx', 'gy', 'gz'))]
  transfers between devices with their start and end apart: 30 -> 30, of which waited for: 14 -> 14; matrix products, arithmetic and copies ran while one was open for 7% -> 5% of each run, Pallas kernels for 0% -> 0%
where the time goes in v1:
time: 997 us; the launch traced here: 987 us
  blocking collectives  618 us (62%)
  local copies, waits for them, and re-layouts  113 us (11%)
  starting transfers between devices  91.5 us (9%)
  matrix products  67.5 us (7%)
  other arithmetic  65.5 us (7%)
  waiting for transfers between devices  30.2 us (3%)
    all_gather x2, blocking collectives, _rest_windows(): inter = jnp.sum(lax.all_gather(view, axis_id), axis=0)  353 us
    psum x2, blocking collectives, body(): lax.psum((local_gram(direction, image, count), local_gram(direction, resi...  138 us
    psum x2, blocking collectives, body(): img_new = lax.psum(local_gram(image, residual, count), ('gx', 'gy', 'gz'))  127 us
    ppermute x15, starting transfers between devices, with_halo(): lax.ppermute(lax.slice_in_dim(block, block.shape[dim] - width, None, axis...  63.7 us
    add x4, other arithmetic, laplace(): total = total + 0.5 * (conduct_mid + face_dif) * (centre - beside)  41.7 us
    dot_general x8, matrix products, combine(): jnp.dot(matrix, flat, precision=lax.Precision.HIGHEST).reshape(fields.shape)  33.2 us
    slice x12, local copies, waits for them, and re-layouts, with_halo(): lax.slice_in_dim(block, 0, width, axis=dim)  32.8 us
    dot_general x8, matrix products, local_gram(): jnp.dot(first.reshape(first.shape[0], -1), second.reshape(second.shape[0]...  32.4 us
  transfers between devices with their start and end apart: 30, of which 14 were waited for; matrix products, arithmetic and copies ran while one was open for 5% of the time, Pallas kernels for 0%

profile of v1, /device:TPU:1, one launch (start us, length us, event | category | flops | bytes accessed | tf_op | source)
XLA Modules:
  0.0 987.3 jit_solution(10976028150490434756)
XLA Ops:
  27.1 4.6 collective-permute-start.9
  32.0 9.8 collective-permute-start.4
  43.7 4.8 collective-permute-done.4
  48.5 4.9 collective-permute-done.5
  69.7 5.1 collective-permute-start.11
  79.1 4.1 copy.528
  83.2 8.6 fusion.64
  100.7 4.3 collective-permute-start.15
  123.1 5.1 collective-permute-start.17
  128.3 6.3 fusion.139
  137.5 4.2 copy.536
  141.7 4.1 copy.538
  145.7 12.2 %fusion.46 = f32[16,16,16,128]{3,2,1,0:T(8,128)S(1)} fusion(f32[16,16,16,128]{3,2,1,0:T(8,128)} %copy-done.4, f32[16,18,18,1]{3,2,1,0:T(8,128)} %copy.538, f32[16,18,1,128]{3,2,1,0:T(1,128)S(1)} %copy.530, f32[16,18,1,128]{3,2,1,0:T(1,128)S(1)} %copy.532, f32[16,1,16,128]{3,2,1,0:T(8,128)S(1)} %collective-permute-done.12, f32[16,1,16,128]{3,2,1,0:T(8,128)} %copy-done.24, ...), kind=kLoop, calls=%fused_computation.83 | loop fusion | flops 19398656 | bytes 5710336 | tf_op jit(solution)/shard_map/add | solution.py:47
  157.9 4.8 fusion.149
  165.7 72.3 %all-reduce.1 = (f32[16,16]{1,0:T(8,128)S(1)}, f32[16,16]{0,1:T(8,128)S(1)}) all-reduce(f32[16,16]{1,0:T(8,128)S(1)} %fusion.139, f32[16,16]{0,1:T(8,128)S(1)} %fusion.149), channel_id=1, replica_groups=mesh['gx'=4,'gy'=8,'gz'=4] {'gx','gy','gz'}, use_global_device_ids=true, to_apply=%region_3.0 | all-reduce | flops 512 | bytes 4096 | tf_op jit(solution)/shard_map/psum | solution.py:93
  242.5 6.2 copy_subtract_fusion
  252.3 63.0 %psum.44 = f32[16,16]{1,0:T(8,128)S(1)} all-reduce(f32[16,16]{1,0:T(8,128)S(1)} %fusion.154), channel_id=1, replica_groups=mesh['gx'=4,'gy'=8,'gz'=4] {'gx','gy','gz'}, use_global_device_ids=true, to_apply=%region_4.8 | all-reduce | flops 256 | bytes 2048 | tf_op jit(solution)/shard_map/psum | solution.py:101
  315.7 4.4 fusion.103
  325.1 176.6 %all-gather = f32[2048,16]{1,0:T(8,128)S(1)} all-gather(f32[16,16]{1,0:T(8,128)S(1)} %fusion.134), channel_id=2, replica_groups=mesh['gx'=4,'gy'=8,'gz'=4] {'gx','gy','gz'}, dimensions={0}, use_global_device_ids=true | all-gather | bytes 132096 | tf_op jit(solution)/shard_map/all_gather | solution.py:11
  506.1 4.4 fusion.5
  536.0 4.1 collective-permute-start.22
  551.1 4.1 copy.566
  555.2 9.5 fusion.28
  574.3 4.1 collective-permute-start.27
  589.3 4.2 collective-permute-start.28
  601.5 5.0 fusion.130
  614.6 11.4 %fusion.10 = f32[16,16,16,128]{3,2,1,0:T(8,128)S(1)} fusion(f32[16,16,16,128]{3,2,1,0:T(8,128)} %copy-done.3, f32[16,18,18,1]{3,2,1,0:T(8,128)} %copy.576, f32[16,18,1,128]{3,2,1,0:T(1,128)S(1)} %copy.568, f32[16,18,1,128]{3,2,1,0:T(1,128)S(1)} %copy.570, f32[16,1,16,128]{3,2,1,0:T(8,128)S(1)} %collective-permute-done.24, f32[16,1,16,128]{3,2,1,0:T(8,128)} %copy-done.23, ...), kind=kLoop, calls=%fused_computation.19 | loop fusion | flops 19398656 | bytes 5710336 | tf_op jit(solution)/shard_map/add | solution.py:47
  632.6 65.8 %all-reduce = (f32[16,16]{1,0:T(8,128)S(1)}, f32[16,16]{1,0:T(8,128)S(1)}) all-reduce(f32[16,16]{1,0:T(8,128)S(1)} %fusion.130, f32[16,16]{1,0:T(8,128)S(1)} %fusion.127), channel_id=1, replica_groups=mesh['gx'=4,'gy'=8,'gz'=4] {'gx','gy','gz'}, use_global_device_ids=true, to_apply=%region_7.11 | all-reduce | flops 512 | bytes 4096 | tf_op jit(solution)/shard_map/psum | solution.py:93
  703.1 5.2 fusion.108
  713.2 63.7 %psum.47 = f32[16,16]{1,0:T(8,128)S(1)} all-reduce(f32[16,16]{1,0:T(8,128)S(1)} %fusion.136), channel_id=1, replica_groups=mesh['gx'=4,'gy'=8,'gz'=4] {'gx','gy','gz'}, use_global_device_ids=true, to_apply=%region_8.12 | all-reduce | flops 256 | bytes 2048 | tf_op jit(solution)/shard_map/psum | solution.py:101
  792.3 176.2 %all-gather.1 = f32[2048,16]{1,0:T(8,128)S(1)} all-gather(f32[16,16]{1,0:T(8,128)S(1)} %fusion.133), channel_id=3, replica_groups=mesh['gx'=4,'gy'=8,'gz'=4] {'gx','gy','gz'}, dimensions={0}, use_global_device_ids=true | all-gather | bytes 132096 | tf_op jit(solution)/shard_map/all_gather | solution.py:11
  980.1 5.0 copy_add_fusion.1
  (238 shorter events, 217.4 us)
Async XLA Ops:
  1.6 5.3 collective-permute-start
  5.6 4.7 collective-permute-start.1
  11.2 9.9 %collective-permute-start.2 = (f32[2,20,2,128]{3,2,1,0:T(2,128)S(1)}, f32[2,20,2,128]{3,2,1,0:T(2,128)S(1)}, u32[]{:S(2)}, u32[]{:S(2)}) collective-permute-start(f32[2,20,2,128]{3,2,1,0:T(2,128)S(1)} %get-tuple-element.66), channel_id=1, source_target_pairs={{0,4},{4,8},{8,12},{12,16},{16,20},{20,24},{24,28},{1,5},{5,9},{9,... | collective-permute-start | bytes 122888 | tf_op jit(solution)/shard_map/ppermute | solution.py:23
  14.3 6.8 collective-permute-start.3
  16.6 5.6 collective-permute-start.7
  19.9 5.7 collective-permute-start.6
  22.9 30.5 %copy-start.17 = (f32[16,16,128]{2,1,0:T(8,128)S(1)}, f32[16,16,128]{2,1,0:T(8,128)}, u32[]{:S(2)}) copy-start(f32[16,16,128]{2,1,0:T(8,128)} %param.14) | copy-start | bytes 393220
  25.8 28.0 %collective-permute-start.8 = (f32[16,18,1,128]{3,0,2,1:T(8,128)S(1)}, f32[16,18,1,128]{3,0,2,1:T(8,128)S(1)}, u32[]{:S(2)}, u32[]{:S(2)}) collective-permute-start(f32[16,18,1,128]{3,0,2,1:T(8,128)S(1)} %copy.606), channel_id=1, source_target_pairs={{4,0},{8,4},{12,8},{16,12},{20,16},{24,20},{28,24},{5,1},{9,5},{13... | collective-permute-start | bytes 442376 | tf_op jit(solution)/shard_map/ppermute | solution.py:26
  27.1 26.8 %collective-permute-start.9 = (f32[16,18,1,128]{3,0,2,1:T(8,128)S(1)}, f32[16,18,1,128]{3,0,2,1:T(8,128)S(1)}, u32[]{:S(2)}, u32[]{:S(2)}) collective-permute-start(f32[16,18,1,128]{3,0,2,1:T(8,128)S(1)} %copy.607), channel_id=1, source_target_pairs={{0,4},{4,8},{8,12},{12,16},{16,20},{20,24},{24,28},{1,5},{5,9},{9,... | collective-permute-start | bytes 442376 | tf_op jit(solution)/shard_map/ppermute | solution.py:23
  32.0 16.5 %collective-permute-start.4 = (f32[2,20,20,2]{3,2,1,0:T(8,128)S(1)}, f32[2,20,20,2]{3,2,1,0:T(8,128)S(1)}, u32[]{:S(2)}, u32[]{:S(2)}) collective-permute-start(f32[2,20,20,2]{3,2,1,0:T(8,128)S(1)} %get-tuple-element.58), channel_id=1, source_target_pairs={{0,1},{1,2},{2,3},{4,5},{5,6},{6,7},{8,9},{9,10},{10,11},{12,13},{... | collective-permute-start | bytes 19208 | tf_op jit(solution)/shard_map/ppermute | solution.py:23
  41.7 11.7 %collective-permute-start.5 = (f32[2,20,20,2]{3,2,1,0:T(8,128)S(1)}, f32[2,20,20,2]{3,2,1,0:T(8,128)S(1)}, u32[]{:S(2)}, u32[]{:S(2)}) collective-permute-start(f32[2,20,20,2]{3,2,1,0:T(8,128)S(1)} %get-tuple-element.59), channel_id=1, source_target_pairs={{1,0},{2,1},{3,2},{5,4},{6,5},{7,6},{9,8},{10,9},{11,10},{13,12},{... | collective-permute-start | bytes 19208 | tf_op jit(solution)/shard_map/ppermute | solution.py:26
  63.8 11.3 %collective-permute-start.10 = (f32[16,18,18,1]{2,0,3,1:T(8,128)}, f32[16,18,18,1]{2,0,3,1:T(8,128)}, u32[]{:S(2)}, u32[]{:S(2)}) collective-permute-start(f32[16,18,18,1]{2,0,3,1:T(8,128)} %copy.525), channel_id=1, source_target_pairs={{1,0},{2,1},{3,2},{5,4},{6,5},{7,6},{9,8},{10,9},{11,10},{13,12},{... | collective-permute-start | bytes 62216 | tf_op jit(solution)/shard_map/ppermute | solution.py:26
  69.7 9.4 collective-permute-start.11
  91.8 5.7 collective-permute-start.12
  93.1 6.0 collective-permute-start.13
  99.3 7.0 collective-permute-start.14
  100.7 7.4 collective-permute-start.15
  116.8 20.8 %collective-permute-start.16 = (f32[16,18,18,1]{2,0,3,1:T(8,128)}, f32[16,18,18,1]{2,0,3,1:T(8,128)}, u32[]{:S(2)}, u32[]{:S(2)}) collective-permute-start(f32[16,18,18,1]{2,0,3,1:T(8,128)} %copy.535), channel_id=1, source_target_pairs={{1,0},{2,1},{3,2},{5,4},{6,5},{7,6},{9,8},{10,9},{11,10},{13,12},{... | collective-permute-start | bytes 62216 | tf_op jit(solution)/shard_map/ppermute | solution.py:26
  123.1 18.5 %collective-permute-start.17 = (f32[16,18,18,1]{2,0,3,1:T(8,128)}, f32[16,18,18,1]{2,0,3,1:T(8,128)}, u32[]{:S(2)}, u32[]{:S(2)}) collective-permute-start(f32[16,18,18,1]{2,0,3,1:T(8,128)} %copy.537), channel_id=1, source_target_pairs={{0,1},{1,2},{2,3},{4,5},{5,6},{6,7},{8,9},{9,10},{10,11},{12,13},{... | collective-permute-start | bytes 62216 | tf_op jit(solution)/shard_map/ppermute | solution.py:23
  248.7 67.0 %copy-start.1 = (f32[16,16,16,128]{3,0,2,1:T(8,128)}, f32[16,16,16,128]{3,0,2,1:T(8,128)S(1)}, u32[]{:S(2)}) copy-start(f32[16,16,16,128]{3,0,2,1:T(8,128)S(1)} %copy_subtract_fusion) | copy-start | bytes 6291460
  510.9 4.2 collective-permute-start.19
  512.3 6.8 collective-permute-start.18
  519.9 6.3 collective-permute-start.20
  521.3 6.1 collective-permute-start.21
  536.0 11.0 %collective-permute-start.22 = (f32[16,18,18,1]{2,0,3,1:T(8,128)}, f32[16,18,18,1]{2,0,3,1:T(8,128)}, u32[]{:S(2)}, u32[]{:S(2)}) collective-permute-start(f32[16,18,18,1]{2,0,3,1:T(8,128)} %copy.563), channel_id=1, source_target_pairs={{1,0},{2,1},{3,2},{5,4},{6,5},{7,6},{9,8},{10,9},{11,10},{13,12},{... | collective-permute-start | bytes 62216 | tf_op jit(solution)/shard_map/ppermute | solution.py:26
  544.1 7.0 collective-permute-start.23
  564.7 7.1 collective-permute-start.24
  566.3 6.5 collective-permute-start.25
  573.0 7.4 collective-permute-start.26
  574.3 6.3 collective-permute-start.27
  589.3 17.2 %collective-permute-start.28 = (f32[16,18,18,1]{2,0,3,1:T(8,128)}, f32[16,18,18,1]{2,0,3,1:T(8,128)}, u32[]{:S(2)}, u32[]{:S(2)}) collective-permute-start(f32[16,18,18,1]{2,0,3,1:T(8,128)} %copy.573), channel_id=1, source_target_pairs={{1,0},{2,1},{3,2},{5,4},{6,5},{7,6},{9,8},{10,9},{11,10},{13,12},{... | collective-permute-start | bytes 62216 | tf_op jit(solution)/shard_map/ppermute | solution.py:26
  597.5 13.1 %collective-permute-start.29 = (f32[16,18,18,1]{2,0,3,1:T(8,128)}, f32[16,18,18,1]{2,0,3,1:T(8,128)}, u32[]{:S(2)}, u32[]{:S(2)}) collective-permute-start(f32[16,18,18,1]{2,0,3,1:T(8,128)} %copy.575), channel_id=1, source_target_pairs={{0,1},{1,2},{2,3},{4,5},{5,6},{6,7},{8,9},{9,10},{10,11},{12,13},{... | collective-permute-start | bytes 62216 | tf_op jit(solution)/shard_map/ppermute | solution.py:23
  (27 other events, 227.3 us)
